TPU v7x, 512 devices: a whole 4x8x8 slice. The times are simulated.
512 devices in a mesh: ctx: 64 (over z, x, core), head: 8 (over y).
Axes of the slice: x: 4, y: 8, z: 8, core: 2. Of those that a mesh axis runs over, the one named last changes fastest.
Arguments:
- queries: bfloat16 [24576, 64, 128], P(('ctx', 'head')), may hold values from -6 to 6
- keys: bfloat16 [24576, 64, 128], P(('ctx', 'head')), may hold values from -6 to 6
- values: bfloat16 [24576, 64, 128], P(('ctx', 'head')), may hold values from -6 to 6
- decay_log: bfloat16 [24576, 64], P(('ctx', 'head')), may hold values from -1 to 0, as said below
- out_gain: float32 [64, 128], replicated, may hold values from 0.1 to 1.9
Outputs:
- normed: bfloat16 [24576, 64, 128], P(('ctx', 'head'))
Inputs may be any that keep to these rules, and one draw needn't show every extreme that they name: `decay_log`: every entry is negative or zero.
All inputs are finite; a program needn't handle non-finite values.
Results may differ from a plain program's by a relative error of at most 0.01.
Values may be sent and summed in bfloat16 or wider, within the bound.
No kernel may reach another device: no remote copies, remote signals or barrier semaphores. Data moves between devices by JAX's collectives and lax.ppermute only.
A program may use at most 128 MiB of HBM per device.

v0:
```python
import jax
import jax.numpy as jnp
from jax import lax
from jax.sharding import PartitionSpec as P


def prefix_2(part, axis, combine, identity):
    place = lax.axis_index(axis)
    gathered = jax.tree.map(lambda a: lax.all_gather(a, axis), part)
    state = jax.tree.map(lambda a, e: jnp.zeros_like(a) + jnp.asarray(e, a.dtype), part, identity)

    def one(step, state):
        return combine(
            state, jax.tree.map(lambda a: lax.dynamic_index_in_dim(a, step, 0, False), gathered)
        )

    return lax.fori_loop(0, place, one, state)


def activate(block):
    return jax.nn.silu(block.astype(jnp.float32)).astype(jnp.bfloat16)


def join_states(earlier, later):
    return (earlier[0] + later[0], jnp.exp(later[0])[:, None, None] * earlier[1] + later[1])


def empty_pair(pair):
    return (jnp.zeros_like(pair[0]), jnp.zeros_like(pair[1]))


def prefix_whole(pair):
    return prefix_2(pair, "ctx", join_states, empty_pair(pair))


def attend(pieces, prefix):
    queries_x, keys_x, values_x, decay_x = pieces
    query_act = activate(queries_x[:, 0])
    key_act = activate(keys_x[:, 0])
    value_act = activate(values_x[:, 0])
    decays = decay_x[:, 0].astype(jnp.float32)
    length = query_act.shape[0]
    token_position_index = lax.iota(jnp.int32, length)
    causal = token_position_index[:, None] >= token_position_index[None, :]
    lower_tri = causal.astype(jnp.float32)
    cumulative = jnp.dot(lower_tri, decays, precision=lax.Precision.HIGHEST)
    scores = jnp.einsum("thd,shd->hts", query_act, key_act, preferred_element_type=jnp.float32)
    offsets = cumulative.T[:, :, None] - cumulative.T[:, None, :]
    causal_heads = causal[None]
    weights = jnp.where(
        causal_heads, scores * jnp.exp(jnp.where(causal_heads, offsets, -1e30)), 0.0
    )
    weights = weights.astype(jnp.bfloat16)
    intra_out = jnp.einsum("hts,shd->thd", weights, value_act, preferred_element_type=jnp.float32)
    ending = cumulative[-1]
    scaled_keys = (
        key_act.astype(jnp.float32) * jnp.exp(ending[None, :] - cumulative)[:, :, None]
    ).astype(jnp.bfloat16)
    local_state = jnp.einsum(
        "shd,she->hde", scaled_keys, value_act, preferred_element_type=jnp.float32
    )
    incoming = prefix((ending, local_state))[1]
    inter_out = jnp.einsum(
        "thd,hde->the", query_act, incoming.astype(jnp.bfloat16), preferred_element_type=jnp.float32
    )
    inter_out = inter_out * jnp.exp(cumulative)[:, :, None]
    return (intra_out + inter_out).astype(jnp.bfloat16)[:, None]


def normalize(mixed, out_gain):
    values32 = mixed.astype(jnp.float32)
    meansq = jnp.mean(values32 * values32, axis=(1, 2), keepdims=True)
    return (values32 * lax.rsqrt(meansq + 1e-06) * out_gain[None]).astype(jnp.bfloat16)


def shards(queries, keys, values, decay_log, out_gain):
    row_count, heads, head_dim = queries.shape
    groups = lax.axis_size("head")
    per_group = heads // groups
    queries_g = queries.reshape(row_count, groups, per_group, head_dim)
    keys_g = keys.reshape(row_count, groups, per_group, head_dim)
    values_g = values.reshape(row_count, groups, per_group, head_dim)
    decay_g = decay_log.reshape(row_count, groups, per_group)
    pieces = (
        lax.all_to_all(queries_g, "head", split_axis=1, concat_axis=0, tiled=True),
        lax.all_to_all(keys_g, "head", split_axis=1, concat_axis=0, tiled=True),
        lax.all_to_all(values_g, "head", split_axis=1, concat_axis=0, tiled=True),
        lax.all_to_all(decay_g, "head", split_axis=1, concat_axis=0, tiled=True),
    )
    attended = attend(pieces, prefix_whole)
    returned = lax.all_to_all(attended, "head", split_axis=0, concat_axis=1, tiled=True)
    mixed = returned.reshape(row_count, heads, head_dim)
    return normalize(mixed, out_gain)


def solution(mesh):
    return jax.shard_map(
        shards,
        mesh=mesh,
        in_specs=(
            P(("ctx", "head"), None, None),
            P(("ctx", "head"), None, None),
            P(("ctx", "head"), None, None),
            P(("ctx", "head"), None),
            P(),
        ),
        out_specs=P(("ctx", "head"), None, None),
        check_vma=False,
    )
```

profile of v0, /device:TPU:455, one launch (start us, length us, event | category | flops | bytes accessed | tf_op | source)
XLA Modules:
  0.0 335.5 jit_solution(378257741241177377)
XLA Ops:
  8.0 6.8 %all-to-all-start.3 = ((bf16[8,2,192]{2,1,0:T(2,128)(2,1)}), bf16[8,2,192]{2,1,0:T(2,128)(2,1)S(1)}, u32[]{:S(2)}, u32[]{:S(2)}) async-start(bf16[8,2,192]{2,1,0:T(2,128)(2,1)} %reshape.86), calls=%async_computation.3 | async-start | bytes 16384 | tf_op jit(solution)/shard_map/all_to_all | solution.py:88
  14.9 2.2 copy.69
  17.1 4.3 %all-to-all-done.3 = bf16[8,2,192]{2,1,0:T(2,128)(2,1)S(1)} async-done(((bf16[8,2,192]{2,1,0:T(2,128)(2,1)}), bf16[8,2,192]{2,1,0:T(2,128)(2,1)S(1)}, u32[]{:S(2)}, u32[]{:S(2)}) %all-to-all-start.3) | async-done | bytes 6176 | tf_op jit(solution)/shard_map/all_to_all | solution.py:88
  21.4 3.5 %all-to-all-start.2 = ((bf16[48,8,8,128]{3,2,0,1:T(8,128)(2,1)}), bf16[48,8,8,128]{3,2,0,1:T(8,128)(2,1)S(1)}, u32[]{:S(2)}, u32[]{:S(2)}) async-start(bf16[48,8,8,128]{3,2,0,1:T(8,128)(2,1)} %copy.69), calls=%async_computation.2 | async-start | bytes 1572864 | tf_op jit(solution)/shard_map/all_to_all | solution.py:86
  26.0 20.7 %all-to-all-done.2 = bf16[48,8,8,128]{3,2,0,1:T(8,128)(2,1)S(1)} async-done(((bf16[48,8,8,128]{3,2,0,1:T(8,128)(2,1)}), bf16[48,8,8,128]{3,2,0,1:T(8,128)(2,1)S(1)}, u32[]{:S(2)}, u32[]{:S(2)}) %all-to-all-start.2) | async-done | bytes 786464 | tf_op jit(solution)/shard_map/all_to_all | solution.py:86
  46.8 3.5 %all-to-all-start = ((bf16[48,8,8,128]{3,2,0,1:T(8,128)(2,1)}), bf16[48,8,8,128]{3,2,0,1:T(8,128)(2,1)S(1)}, u32[]{:S(2)}, u32[]{:S(2)}) async-start(bf16[48,8,8,128]{3,2,0,1:T(8,128)(2,1)} %copy.63), calls=%async_computation | async-start | bytes 1572864 | tf_op jit(solution)/shard_map/all_to_all | solution.py:87
  51.1 20.8 %all-to-all-done = bf16[48,8,8,128]{3,2,0,1:T(8,128)(2,1)S(1)} async-done(((bf16[48,8,8,128]{3,2,0,1:T(8,128)(2,1)}), bf16[48,8,8,128]{3,2,0,1:T(8,128)(2,1)S(1)}, u32[]{:S(2)}, u32[]{:S(2)}) %all-to-all-start) | async-done | bytes 786464 | tf_op jit(solution)/shard_map/all_to_all | solution.py:87
  73.2 2.2 fusion.13
  76.5 3.5 %all-to-all-start.1 = ((bf16[48,8,8,128]{3,2,0,1:T(8,128)(2,1)}), bf16[48,8,8,128]{3,2,0,1:T(8,128)(2,1)S(1)}, u32[]{:S(2)}, u32[]{:S(2)}) async-start(bf16[48,8,8,128]{3,2,0,1:T(8,128)(2,1)} %copy.66), calls=%async_computation.1 | async-start | bytes 1572864 | tf_op jit(solution)/shard_map/all_to_all | solution.py:85
  80.1 38.4 %all-gather.1 = f32[64,1,8]{2,1,0:T(1,128)S(1)} all-gather(f32[1,1,8]{2,1,0:T(1,128)S(1)} %bitcast.88), channel_id=1, replica_groups=mesh['ctx'=64,'head'=8] {'ctx'}, dimensions={0}, use_global_device_ids=true | all-gather | bytes 2080 | tf_op jit(solution)/shard_map/all_gather | solution.py:9
  118.6 6.0 %fusion = f32[8,128,384]{2,1,0:T(8,128)} fusion(f32[8,384]{1,0:T(8,128)S(1)} %bitcast.87, pred[384,384]{1,0:T(8,128)(4,1)S(1)} %iota_compare_fusion, f32[384,8,128]{2,1,0:T(8,128)S(1)} %bitcast.76, f32[384,8,128]{2,1,0:T(8,128)} %bitcast.81, f32[384,8,128]{2,1,0:T(8,128)} %bitcast.79), kind=kOutput, calls=%fused_computation.3 | convolution fusion | flops 615776256 | bytes 6451200 | tf_op jit(solution)/shard_map/hts,shd->thd/dot_general | solution.py:54
  124.6 91.6 %all-gather.4.cloned.1.call-done = f32[512,128,128]{2,1,0:T(8,128)} async-done(((f32[8,128,128]{2,1,0:T(8,128)}), f32[512,128,128]{2,1,0:T(8,128)}) %all-gather.4.cloned.1.call-update) | async-done | bytes 33554448 | tf_op jit(solution)/shard_map/all_gather | solution.py:9
  216.2 77.7 %while.12 = (s32[]{:T(128)}, f32[8,128,128]{2,1,0:T(8,128)S(1)}, s32[]{:T(128)}, f32[64,8]{1,0:T(8,128)S(1)}, f32[64,8,128,128]{3,2,1,0:T(8,128)}, /*index=5*/s32[]{:T(128)}, s32[]{:T(128)}, s32[]{:T(128)}) while((s32[]{:T(128)}, f32[8,128,128]{2,1,0:T(8,128)S(1)}, s32[]{:T(128)}, f32[64,8]{1,0:T(8,128)S(1)}, f32[64,8,128,128]{3,2,1,0:T(8,128)}, ...), condition=%wide.region_1.2_spmd, body=%wide.region_0.1_spmd.sunk | while | flops 262149 | bytes 1573095 | solution.py:17
  216.3 1.2 bitcast_add_fusion.2
  217.5 1.2 bitcast_add_fusion.2
  218.7 1.2 bitcast_add_fusion.2
  220.0 1.2 bitcast_add_fusion.2
  221.2 1.2 bitcast_add_fusion.2
  222.4 1.2 bitcast_add_fusion.2
  223.7 1.2 bitcast_add_fusion.2
  224.9 1.2 bitcast_add_fusion.2
  226.1 1.2 bitcast_add_fusion.2
  227.3 1.2 bitcast_add_fusion.2
  228.6 1.2 bitcast_add_fusion.2
  229.8 1.2 bitcast_add_fusion.2
  231.0 1.2 bitcast_add_fusion.2
  232.3 1.2 bitcast_add_fusion.2
  233.5 1.2 bitcast_add_fusion.2
  234.7 1.2 bitcast_add_fusion.2
  236.0 1.2 bitcast_add_fusion.2
  237.2 1.2 bitcast_add_fusion.2
  238.4 1.2 bitcast_add_fusion.2
  239.7 1.2 bitcast_add_fusion.2
  240.9 1.2 bitcast_add_fusion.2
  242.1 1.2 bitcast_add_fusion.2
  243.4 1.2 bitcast_add_fusion.2
  244.6 1.2 bitcast_add_fusion.2
  245.8 1.2 bitcast_add_fusion.2
  247.1 1.2 bitcast_add_fusion.2
  248.3 1.2 bitcast_add_fusion.2
  249.5 1.2 bitcast_add_fusion.2
  250.8 1.2 bitcast_add_fusion.2
  252.0 1.2 bitcast_add_fusion.2
  253.2 1.2 bitcast_add_fusion.2
  254.5 1.2 bitcast_add_fusion.2
  255.7 1.2 bitcast_add_fusion.2
  256.9 1.2 bitcast_add_fusion.2
  258.2 1.2 bitcast_add_fusion.2
  259.4 1.2 bitcast_add_fusion.2
  260.6 1.2 bitcast_add_fusion.2
  261.9 1.2 bitcast_add_fusion.2
  263.1 1.2 bitcast_add_fusion.2
  264.3 1.2 bitcast_add_fusion.2
  265.6 1.2 bitcast_add_fusion.2
  266.8 1.2 bitcast_add_fusion.2
  268.0 1.2 bitcast_add_fusion.2
  270.5 1.2 bitcast_add_fusion.2
  273.0 1.2 bitcast_add_fusion.2
  279.1 1.2 bitcast_add_fusion.2
  281.6 1.2 bitcast_add_fusion.2
  287.7 1.2 bitcast_add_fusion.2
  290.2 1.2 bitcast_add_fusion.2
  293.9 2.2 fusion.12
  296.6 29.7 %all_to_all.51 = bf16[384,1,8,128]{3,2,1,0:T(8,128)(2,1)S(1)} all-to-all(bf16[384,1,8,128]{3,2,1,0:T(8,128)(2,1)S(1)} %copy.77), channel_id=1, replica_groups=mesh['ctx'=64,'head'=8] {'head'}, dimensions={0} | all-to-all | bytes 1572864 | tf_op jit(solution)/shard_map/all_to_all | solution.py:91
  (114 shorter events, 26.1 us)
Async XLA Ops:
  8.0 13.4 %all-to-all-start.3 = ((bf16[8,2,192]{2,1,0:T(2,128)(2,1)}), bf16[8,2,192]{2,1,0:T(2,128)(2,1)S(1)}, u32[]{:S(2)}, u32[]{:S(2)}) async-start(bf16[8,2,192]{2,1,0:T(2,128)(2,1)} %reshape.86), calls=%async_computation.3 | async-start | bytes 16384 | tf_op jit(solution)/shard_map/all_to_all | solution.py:88
  14.9 10.1 %copy-start.2 = (bf16[48,64,128]{2,1,0:T(8,128)(2,1)S(1)}, bf16[48,64,128]{2,1,0:T(8,128)(2,1)}, u32[]{:S(2)}) copy-start(bf16[48,64,128]{2,1,0:T(8,128)(2,1)} %param.9) | copy-start | bytes 2359300
  21.4 25.3 %all-to-all-start.2 = ((bf16[48,8,8,128]{3,2,0,1:T(8,128)(2,1)}), bf16[48,8,8,128]{3,2,0,1:T(8,128)(2,1)S(1)}, u32[]{:S(2)}, u32[]{:S(2)}) async-start(bf16[48,8,8,128]{3,2,0,1:T(8,128)(2,1)} %copy.69), calls=%async_computation.2 | async-start | bytes 1572864 | tf_op jit(solution)/shard_map/all_to_all | solution.py:86
  46.8 25.2 %all-to-all-start = ((bf16[48,8,8,128]{3,2,0,1:T(8,128)(2,1)}), bf16[48,8,8,128]{3,2,0,1:T(8,128)(2,1)S(1)}, u32[]{:S(2)}, u32[]{:S(2)}) async-start(bf16[48,8,8,128]{3,2,0,1:T(8,128)(2,1)} %copy.63), calls=%async_computation | async-start | bytes 1572864 | tf_op jit(solution)/shard_map/all_to_all | solution.py:87
  50.3 165.9 %all-gather.4.cloned.1.call-start = ((), (), s32[]{:S(2)}) async-start(), calls=%async_computation.5 | async-start | bytes 34078720 | tf_op jit(solution)/shard_map/all_gather | solution.py:9
  51.1 24.3 %copy-start = (f32[48,8,1,8,128]{4,3,0,1,2:T(8,128)}, f32[48,8,1,8,128]{4,3,0,1,2:T(8,128)S(1)}, u32[]{:S(2)}) copy-start(f32[48,8,1,8,128]{4,3,0,1,2:T(8,128)S(1)} %bitcast_convert_fusion.1) | copy-start | bytes 4718596
  72.1 1.1 copy-start.1
  73.2 2.2 copy-start.3
  76.5 42.0 %all-to-all-start.1 = ((bf16[48,8,8,128]{3,2,0,1:T(8,128)(2,1)}), bf16[48,8,8,128]{3,2,0,1:T(8,128)(2,1)S(1)}, u32[]{:S(2)}, u32[]{:S(2)}) async-start(bf16[48,8,8,128]{3,2,0,1:T(8,128)(2,1)} %copy.66), calls=%async_computation.1 | async-start | bytes 1572864 | tf_op jit(solution)/shard_map/all_to_all | solution.py:85
  326.2 1.3 copy-start.4
Sparse Core Ops, SparseCore 0:
  75.6 140.5 all-gather.3
where the time goes:
time: 339 us; the launch traced here: 335 us
  waiting for transfers between devices  138 us (41%)
  other arithmetic  77.7 us (23%)
  blocking collectives  68 us (20%)
  starting transfers between devices  17.5 us (5%)
  between operations  13.6 us (4%)
  matrix products  10.5 us (3%)
  local copies, waits for them, and re-layouts  8.73 us (3%)
    all_gather x1, waiting for transfers between devices, prefix_2(): gathered = jax.tree.map(lambda a: lax.all_gather(a, axis), part)  91.6 us
    add x63, other arithmetic, join_states(): jnp.exp(later[0])[:, None, None] * earlier[1] + later[1]  75 us
    all_gather x1, blocking collectives, prefix_2(): gathered = jax.tree.map(lambda a: lax.all_gather(a, axis), part)  38.4 us
    all_to_all x1, blocking collectives, shards(): lax.all_to_all(attended, 'head', split_axis=0, concat_axis=1, tiled=True)  29.7 us
    all_to_all x1, waiting for transfers between devices, shards(): lax.all_to_all(values_g, 'head', split_axis=1, concat_axis=0, tiled=True)  20.8 us
    all_to_all x1, waiting for transfers between devices, shards(): lax.all_to_all(keys_g, 'head', split_axis=1, concat_axis=0, tiled=True)  20.7 us
    all_to_all x1, starting transfers between devices, shards(): lax.all_to_all(decay_g, 'head', split_axis=1, concat_axis=0, tiled=True)  6.82 us
  transfers between devices with their start and end apart: 5, of which 4 were waited for; matrix products, arithmetic and copies ran while one was open for 3% of the time, Pallas kernels for 0%

commit v1 on v0

v1 whole, which is shorter than its diff:
```python
import functools

import jax
import jax.numpy as jnp
from jax import lax
from jax.experimental import pallas as pl
from jax.experimental.pallas import tpu as pltpu
from jax.sharding import Mesh
from jax.sharding import PartitionSpec as P

F32 = jnp.float32
BF16 = jnp.bfloat16
EXTRA = 8
LIMIT = 48 * 1024 * 1024


def iota(shape, axis):
    return lax.broadcasted_iota(jnp.int32, shape, axis)


def silu(x):
    half = 0.5 * x
    return half + half * jnp.tanh(half)


def three_parts(x):
    high = x.astype(BF16)
    rest = x - high.astype(F32)
    middle = rest.astype(BF16)
    low = (rest - middle.astype(F32)).astype(BF16)
    return high, middle, low


def dot_parts(mask, parts):
    return sum(jnp.dot(mask, part, preferred_element_type=F32) for part in parts)


def local_cumulative(decay, group):
    tokens, heads = decay.shape
    tril = (iota((tokens, tokens), 0) >= iota((tokens, tokens), 1)).astype(F32).astype(BF16)
    running = jnp.dot(tril, decay, preferred_element_type=F32)
    wide = jnp.concatenate([running, jnp.zeros((tokens, 128 - heads), F32)], axis=1)
    return pltpu.roll(wide, lax.rem(128 - 8 * group, 128), 1)


def pack_kv_kernel(decay_ref, keys_ref, values_ref, out_ref, key_rows, value_rows):
    tokens = keys_ref.shape[0]
    running = local_cumulative(decay_ref[...], pl.program_id(0))
    key_rows[...] = keys_ref[...].astype(F32).reshape(tokens * 8, 128)
    value_rows[...] = values_ref[...].astype(F32).reshape(tokens * 8, 128)
    to_end = jnp.exp(running[tokens - 1 : tokens, :] - running)
    row = iota((EXTRA, 128), 0)
    for j in range(8):
        rows = pl.ds(j, tokens, stride=8)
        scale = jnp.broadcast_to(to_end[:, j : j + 1], (tokens, 128))
        out_ref[j, 0:tokens, :] = (silu(key_rows[rows, :]) * scale).astype(BF16)
        out_ref[j, tokens : 2 * tokens, :] = silu(value_rows[rows, :]).astype(BF16)
        total = jnp.broadcast_to(running[tokens - 1 : tokens, j : j + 1], (EXTRA, 128))
        high, middle, low = (part.astype(F32) for part in three_parts(total))
        out_ref[j, 2 * tokens : 2 * tokens + EXTRA, :] = jnp.where(
            row == 0, high, jnp.where(row == 1, middle, jnp.where(row == 2, low, 0.0))
        ).astype(BF16)


def pack_kv(keys, values, decay):
    tokens, heads, dim = keys.shape
    block = pl.BlockSpec((tokens, 8, dim), lambda g: (0, g, 0))
    return pl.pallas_call(
        pack_kv_kernel,
        grid=(heads // 8,),
        in_specs=[pl.BlockSpec((tokens, heads), lambda g: (0, 0)), block, block],
        out_specs=pl.BlockSpec((8, 2 * tokens + EXTRA, dim), lambda g: (g, 0, 0)),
        out_shape=jax.ShapeDtypeStruct((heads, 2 * tokens + EXTRA, dim), BF16),
        scratch_shapes=[pltpu.VMEM((tokens * 8, dim), F32)] * 2,
        compiler_params=pltpu.CompilerParams(vmem_limit_bytes=LIMIT),
        name="pack_kv",
    )(decay, keys, values)


def pack_q_kernel(decay_ref, queries_ref, out_ref, query_rows):
    tokens = queries_ref.shape[0]
    running = local_cumulative(decay_ref[...], pl.program_id(0))
    query_rows[...] = queries_ref[...].astype(F32).reshape(tokens * 8, 128)
    grown = jnp.exp(running)
    for j in range(8):
        scale = jnp.broadcast_to(grown[:, j : j + 1], (tokens, 128))
        rows = query_rows[pl.ds(j, tokens, stride=8), :]
        out_ref[j] = (silu(rows) * scale).astype(BF16)


def pack_q(queries, decay):
    tokens, heads, dim = queries.shape
    return pl.pallas_call(
        pack_q_kernel,
        grid=(heads // 8,),
        in_specs=[
            pl.BlockSpec((tokens, heads), lambda g: (0, 0)),
            pl.BlockSpec((tokens, 8, dim), lambda g: (0, g, 0)),
        ],
        out_specs=pl.BlockSpec((8, tokens, dim), lambda g: (g, 0, 0)),
        out_shape=jax.ShapeDtypeStruct((heads, tokens, dim), BF16),
        scratch_shapes=[pltpu.VMEM((tokens * 8, dim), F32)],
        compiler_params=pltpu.CompilerParams(vmem_limit_bytes=LIMIT),
        name="pack_q",
    )(decay, queries)


def states_kernel(per_block, kv_ref, prefix_ref, total_ref, factor_ref, enter_ref, reach_ref):
    sources, rows, dim = kv_ref.shape
    tokens = (rows - EXTRA) // 2
    blocks = sources // per_block
    length = per_block * tokens
    tail = kv_ref[:, 2 * tokens : rows, :].astype(F32)
    totals = jnp.sum(tail, axis=1)
    parts = three_parts(totals)
    at, of = iota((sources, sources), 0), iota((sources, sources), 1)
    same = at // per_block == of // per_block

    def mask(keep):
        return keep.astype(F32).astype(BF16)

    before = dot_parts(mask(same & (of < at)), parts)
    after = dot_parts(mask(same & (of > at)), parts)
    enter_ref[...] = jnp.exp(before)
    to_block_end = jnp.exp(after)
    block_at, source_of = iota((blocks, sources), 0), iota((blocks, sources), 1) // per_block
    block_total = dot_parts(mask(block_at == source_of), parts)
    block_before = dot_parts(mask(block_at > source_of), parts)
    reach_ref[...] = jnp.exp(block_before)
    in_lanes = jnp.transpose(totals)[0:blocks, :]
    picked = jnp.where(block_at == source_of, in_lanes, 0.0)
    member, position = iota((sources, length), 0), iota((sources, length), 1)
    up_to = mask(lax.rem(member, per_block) <= position // tokens)
    through = sum(jnp.dot(part, up_to, preferred_element_type=F32) for part in three_parts(picked))
    source_row = iota((per_block, length), 0)
    source_col = iota((per_block, length), 1) // tokens
    repeats = length // dim
    state = jnp.zeros((dim, dim), F32)
    for b in range(blocks):
        here = slice(b * per_block, (b + 1) * per_block)
        start = jnp.concatenate([before[here]] * repeats, axis=1)
        factor_ref[b] = jnp.where(
            source_col <= source_row, jnp.exp(start - through[b : b + 1, :]), 0.0
        )
        prefix_ref[b] = state
        keys = kv_ref[here, 0:tokens, :].astype(F32) * to_block_end[here][:, None, :]
        values = kv_ref[here, tokens : 2 * tokens, :].reshape(length, dim)
        own = lax.dot_general(
            keys.astype(BF16).reshape(length, dim), values, (((0,), (0,)), ((), ())),
            preferred_element_type=F32,
        )
        state = jnp.exp(block_total[b : b + 1, :]) * state + own
    total_ref[0:dim, :] = state
    total_ref[dim : dim + 8, :] = jnp.broadcast_to(
        jnp.sum(block_total, axis=0, keepdims=True), (8, dim)
    )


def states(kv, per_block):
    sources, rows, dim = kv.shape
    blocks, length = sources // per_block, per_block * (rows - EXTRA) // 2
    return pl.pallas_call(
        functools.partial(states_kernel, per_block),
        out_shape=(
            jax.ShapeDtypeStruct((blocks, dim, dim), F32),
            jax.ShapeDtypeStruct((dim + 8, dim), F32),
            jax.ShapeDtypeStruct((blocks, per_block, length), F32),
            jax.ShapeDtypeStruct((sources, dim), F32),
            jax.ShapeDtypeStruct((blocks, dim), F32),
        ),
        compiler_params=pltpu.CompilerParams(vmem_limit_bytes=LIMIT),
        name="states",
    )(kv)


def attend_kernel(query_ref, kv_ref, prefix_ref, factor_ref, enter_ref, reach_ref, incoming_ref, out_ref):
    per_block, tokens, dim = query_ref.shape
    length = per_block * tokens
    b = pl.program_id(0)
    query = query_ref[...].reshape(length, dim)
    key = kv_ref[:, 0:tokens, :].reshape(length, dim)
    value = kv_ref[:, tokens : 2 * tokens, :].reshape(length, dim)
    state = prefix_ref[0] + reach_ref[pl.ds(b, 1), :] * incoming_ref[...]
    inter = jnp.dot(query, state.astype(BF16), preferred_element_type=F32)

    def spread(x):
        return jnp.concatenate(
            [jnp.broadcast_to(x[i : i + 1], (tokens, x.shape[1])) for i in range(per_block)], axis=0
        )

    factor = spread(factor_ref[0])
    enter = spread(enter_ref[...])
    step = 128
    causal = iota((step, step), 0) >= iota((step, step), 1)
    for low in range(0, length, step):
        high = low + step
        scores = lax.dot_general(
            query[low:high], key[0:high], (((1,), (1,)), ((), ())), preferred_element_type=F32
        )
        scores = scores * factor[low:high, 0:high]
        diagonal = jnp.where(causal, scores[:, low:high], 0.0)
        if low:
            scores = jnp.concatenate([scores[:, 0:low], diagonal], axis=1)
        else:
            scores = diagonal
        intra = jnp.dot(scores.astype(BF16), value[0:high], preferred_element_type=F32)
        mixed = (intra + enter[low:high] * inter[low:high]).astype(BF16)
        for i in range(low // 16, high // 16):
            source, row = divmod(i * 16, tokens)
            out_ref[source, row : row + 16, :] = mixed[i * 16 - low : i * 16 - low + 16]


def attend(query, kv, prefix, factor, enter, reach, incoming, per_block):
    sources, tokens, dim = query.shape
    rows = kv.shape[1]
    blocks, length = sources // per_block, per_block * tokens

    def whole(shape):
        return pl.BlockSpec(shape, lambda b: (0,) * len(shape))

    return pl.pallas_call(
        attend_kernel,
        grid=(blocks,),
        in_specs=[
            pl.BlockSpec((per_block, tokens, dim), lambda b: (b, 0, 0)),
            pl.BlockSpec((per_block, rows, dim), lambda b: (b, 0, 0)),
            pl.BlockSpec((1, dim, dim), lambda b: (b, 0, 0)),
            pl.BlockSpec((1, per_block, length), lambda b: (b, 0, 0)),
            pl.BlockSpec((per_block, dim), lambda b: (b, 0)),
            whole((blocks, dim)),
            whole((dim, dim)),
        ],
        out_specs=pl.BlockSpec((per_block, tokens, dim), lambda b: (b, 0, 0)),
        out_shape=jax.ShapeDtypeStruct((sources, tokens, dim), BF16),
        compiler_params=pltpu.CompilerParams(vmem_limit_bytes=LIMIT),
        name="attend",
    )(query, kv, prefix, factor, enter, reach, incoming)


def norm_kernel(mixed_ref, gain_ref, out_ref, rows_ref):
    heads, tokens, dim = mixed_ref.shape
    squares = jnp.zeros((tokens, dim), F32)
    for h in range(heads):
        x = mixed_ref[h].astype(F32)
        squares = squares + x * x
    mean = jnp.sum(squares, axis=1, keepdims=True) * (1.0 / (heads * dim))
    scale = jnp.broadcast_to(lax.rsqrt(mean + 1e-06), (tokens, dim))
    for h in range(heads):
        x = mixed_ref[h].astype(F32) * scale * gain_ref[h : h + 1, :]
        rows_ref[pl.ds(h, tokens, stride=heads), :] = x
    for t in range(tokens):
        out_ref[t] = rows_ref[t * heads : (t + 1) * heads, :].astype(BF16)


def norm(mixed, gain):
    heads, tokens, dim = mixed.shape
    return pl.pallas_call(
        norm_kernel,
        out_shape=jax.ShapeDtypeStruct((tokens, heads, dim), BF16),
        scratch_shapes=[pltpu.VMEM((tokens * heads, dim), F32)],
        compiler_params=pltpu.CompilerParams(vmem_limit_bytes=LIMIT),
        name="norm",
    )(mixed, gain)


def incoming_state(own):
    dim = own.shape[1]
    segment = lax.axis_index("seg")
    count = lax.axis_size("seg")
    whole = own
    entering = jnp.zeros_like(own)

    def join(earlier, later):
        decay = jnp.exp(later[dim : dim + 1])
        return jnp.concatenate([decay * earlier[:dim] + later[:dim], earlier[dim:] + later[dim:]], axis=0)

    hop = 1
    while hop < count // 2:
        other = lax.ppermute(whole, "seg", [(i, i ^ hop) for i in range(count)])
        upper = (segment & hop) != 0
        entering = jnp.where(upper, join(other, entering), entering)
        whole = jnp.where(upper, join(other, whole), join(whole, other))
        hop *= 2
    half = count // 2
    other = lax.ppermute(whole, "seg", [(i, half + (i + half // 2) % half) for i in range(half)])
    return jnp.exp(entering[dim : dim + 1]) * other[:dim] + entering[:dim]


def shards(queries, keys, values, decay_log, out_gain):
    per_block = lax.axis_size("head")
    group = ("sub", "head")
    kv = lax.all_to_all(pack_kv(keys, values, decay_log), group, 0, 0, tiled=True)
    query = lax.all_to_all(pack_q(queries, decay_log), group, 0, 0, tiled=True)
    prefix, total, factor, enter, reach = states(kv, per_block)
    incoming = incoming_state(total)
    mixed = attend(query, kv, prefix, factor, enter, reach, incoming, per_block)
    mixed = lax.all_to_all(mixed, group, 0, 0, tiled=True)
    return norm(mixed, out_gain)


def solution(mesh):
    devices = mesh.devices
    contexts, per_block = devices.shape
    heads = 64
    sub = heads // per_block
    split = Mesh(devices.reshape(contexts // sub, sub, per_block), ("seg", "sub", "head"))
    rows = ("seg", "sub", "head")
    return jax.shard_map(
        shards,
        mesh=split,
        in_specs=(P(rows, None, None), P(rows, None, None), P(rows, None, None), P(rows, None), P()),
        out_specs=P(rows, None, None),
        check_vma=False,
    )
```

time: 339 us -> 136 us (0.40)
  the two profiles are of different devices: /device:TPU:455 before, /device:TPU:1 now
where the time goes in v1:
time: 136 us; the launch traced here: 135 us
  waiting for transfers between devices  43 us (32%)
  starting transfers between devices  36.8 us (27%)
  blocking collectives  35.5 us (26%)
  Pallas kernels  16.4 us (12%)
  local copies, waits for them, and re-layouts  3.01 us (2%)
    all_to_all x1, waiting for transfers between devices, shards(): lax.all_to_all(pack_kv(keys, values, decay_log), group, 0, 0, tiled=True)  37.6 us
    all_to_all x1, blocking collectives, shards(): mixed = lax.all_to_all(mixed, group, 0, 0, tiled=True)  35.5 us
    all_to_all x1, starting transfers between devices, shards(): lax.all_to_all(pack_kv(keys, values, decay_log), group, 0, 0, tiled=True)  11.8 us
    ppermute x2, starting transfers between devices, incoming_state(): other = lax.ppermute(whole, 'seg', [(i, i ^ hop) for i in range(count)])  9.81 us
    ppermute x1, starting transfers between devices, incoming_state(): lax.ppermute(whole, 'seg', [(i, half + (i + half // 2) % half) for i in r...  8.3 us
    all_to_all x1, starting transfers between devices, shards(): query = lax.all_to_all(pack_q(queries, decay_log), group, 0, 0, tiled=True)  6.95 us
    pallas_call x1, Pallas kernels, pack_kv(): pl.pallas_call(pack_kv_kernel, grid=(heads // 8,), in_specs=[pl.BlockSpec...  4.9 us
    pallas_call x1, Pallas kernels, pack_q(): pl.pallas_call(pack_q_kernel, grid=(heads // 8,), in_specs=[pl.BlockSpec(...  4.4 us
  transfers between devices with their start and end apart: 5, of which 4 were waited for; matrix products, arithmetic and copies ran while one was open for 0% of the time, Pallas kernels for 4%

profile of v1, /device:TPU:1, one launch (start us, length us, event | category | flops | bytes accessed | tf_op | source)
XLA Modules:
  0.0 135.0 jit_solution(13834143301463403374)
XLA Ops:
  0.0 0.0 copy-start.1
  0.0 1.1 copy-done.1
  1.1 0.0 copy-start.2
  1.1 1.1 copy-done.2
  2.3 0.0 copy-start.3
  2.3 0.7 copy-done.3
  3.0 4.9 %pack_kv.1 = bf16[64,104,128]{2,1,0:T(8,128)(2,1)} custom-call(bf16[48,64]{1,0:T(8,128)(2,1)S(1)} %copy-done.3, bf16[48,64,128]{2,1,0:T(8,128)(2,1)S(1)} %copy-done.1, bf16[48,64,128]{2,1,0:T(8,128)(2,1)S(1)} %copy-done.2), custom_call_target="tpu_custom_call" | custom-call | tf_op jit(solution)/shard_map/pack_kv/pallas_call | solution.py:68
  7.9 0.0 copy-start
  7.9 0.0 copy-start.4
  7.9 11.8 %all-to-all-start.1 = ((bf16[64,104,128]{2,1,0:T(8,128)(2,1)}), bf16[64,104,128]{2,1,0:T(8,128)(2,1)S(1)}, u32[]{:S(2)}, u32[]{:S(2)}) async-start(bf16[64,104,128]{2,1,0:T(8,128)(2,1)} %pack_kv.1), calls=%async_computation.1 | async-start | bytes 3407872 | tf_op jit(solution)/shard_map/all_to_all | solution.py:292
  19.7 0.0 copy-done
  19.7 0.0 copy-done.4
  19.7 4.4 %pack_q.1 = bf16[64,48,128]{2,1,0:T(8,128)(2,1)} custom-call(bf16[48,64]{1,0:T(8,128)(2,1)S(1)} %copy-done.4, bf16[48,64,128]{2,1,0:T(8,128)(2,1)S(1)} %copy-done), custom_call_target="tpu_custom_call" | custom-call | tf_op jit(solution)/shard_map/pack_q/pallas_call | solution.py:93
  24.1 37.6 %all-to-all-done.1.kv_ref = bf16[64,104,128]{2,1,0:T(8,128)(2,1)S(1)} async-done(((bf16[64,104,128]{2,1,0:T(8,128)(2,1)}), bf16[64,104,128]{2,1,0:T(8,128)(2,1)S(1)}, u32[]{:S(2)}, u32[]{:S(2)}) %all-to-all-start.1) | async-done | bytes 1703968 | tf_op jit(solution)/shard_map/all_to_all | solution.py:292
  61.7 6.9 %all-to-all-start = ((bf16[64,48,128]{2,1,0:T(8,128)(2,1)}), bf16[64,48,128]{2,1,0:T(8,128)(2,1)S(1)}, u32[]{:S(2)}, u32[]{:S(2)}) async-start(bf16[64,48,128]{2,1,0:T(8,128)(2,1)} %pack_q.1), calls=%async_computation | async-start | bytes 1572864 | tf_op jit(solution)/shard_map/all_to_all | solution.py:293
  68.6 0.7 states.1
  69.4 4.0 %collective-permute-start = (f32[136,128]{1,0:T(8,128)S(1)}, f32[136,128]{1,0:T(8,128)S(1)}, u32[]{:S(2)}, u32[]{:S(2)}) collective-permute-start(f32[136,128]{1,0:T(8,128)S(1)} %get-tuple-element.14), channel_id=1, source_target_pairs={{0,64},{64,0},{128,192},{192,128},{256,320},{320,256},{384,448},{4... | collective-permute-start | bytes 208904 | tf_op jit(solution)/shard_map/ppermute | solution.py:279
  73.4 2.1 %collective-permute-done = f32[136,128]{1,0:T(8,128)S(1)} collective-permute-done((f32[136,128]{1,0:T(8,128)S(1)}, f32[136,128]{1,0:T(8,128)S(1)}, u32[]{:S(2)}, u32[]{:S(2)}) %collective-permute-start) | collective-permute-done | bytes 69664 | tf_op jit(solution)/shard_map/ppermute | solution.py:279
  75.6 5.8 %collective-permute-start.1 = (f32[136,128]{1,0:T(8,128)S(1)}, f32[136,128]{1,0:T(8,128)S(1)}, u32[]{:S(2)}, u32[]{:S(2)}) collective-permute-start(f32[136,128]{1,0:T(8,128)S(1)} %fusion.1), channel_id=1, source_target_pairs={{0,128},{64,192},{128,0},{192,64},{256,384},{320,448},{384,256},{4... | collective-permute-start | bytes 208904 | tf_op jit(solution)/shard_map/ppermute | solution.py:279
  81.4 1.9 %collective-permute-done.1 = f32[136,128]{1,0:T(8,128)S(1)} collective-permute-done((f32[136,128]{1,0:T(8,128)S(1)}, f32[136,128]{1,0:T(8,128)S(1)}, u32[]{:S(2)}, u32[]{:S(2)}) %collective-permute-start.1) | collective-permute-done | bytes 69664 | tf_op jit(solution)/shard_map/ppermute | solution.py:279
  83.4 8.3 %collective-permute-start.2 = (f32[136,128]{1,0:T(8,128)S(1)}, f32[136,128]{1,0:T(8,128)S(1)}, u32[]{:S(2)}, u32[]{:S(2)}) collective-permute-start(f32[136,128]{1,0:T(8,128)S(1)} %fusion), channel_id=1, source_target_pairs={{0,384},{64,448},{128,256},{192,320},{1,385},{65,449},{129,257},{1... | collective-permute-start | bytes 208904 | tf_op jit(solution)/shard_map/ppermute | solution.py:285
  91.8 1.3 collective-permute-done.2
  93.1 0.0 all-to-all-done.query_ref
  93.1 0.0 copy-start.5
  93.1 3.9 %attend.1 = bf16[64,48,128]{2,1,0:T(8,128)(2,1)S(1)} custom-call(bf16[64,48,128]{2,1,0:T(8,128)(2,1)S(1)} %all-to-all-done.query_ref, bf16[64,104,128]{2,1,0:T(8,128)(2,1)S(1)} %all-to-all-done.1.kv_ref, f32[8,128,128]{2,1,0:T(8,128)S(1)} %get-tuple-element.10.prefix_ref, f32[8,8,384]{2,1,0:T(8,128)S(1)} %get-tuple-element.11.factor_ref, ...), custom_call_target="tpu_custom_call" | custom-call | tf_op jit(solution)/shard_map/attend/pallas_call | solution.py:221
  97.1 35.5 %all_to_all.15.mixed_ref = bf16[64,48,128]{2,1,0:T(8,128)(2,1)S(1)} all-to-all(bf16[64,48,128]{2,1,0:T(8,128)(2,1)S(1)} %attend.1), channel_id=1, replica_groups=mesh['seg'=8,'sub'=8,'head'=8] {'sub','head'}, dimensions={0} | all-to-all | bytes 1572864 | tf_op jit(solution)/shard_map/all_to_all | solution.py:297
  132.5 0.0 copy-done.5
  132.5 2.5 %norm.1 = bf16[48,64,128]{2,1,0:T(8,128)(2,1)} custom-call(bf16[64,48,128]{2,1,0:T(8,128)(2,1)S(1)} %all_to_all.15.mixed_ref, f32[64,128]{1,0:T(8,128)S(1)} %copy-done.5), custom_call_target="tpu_custom_call" | custom-call | tf_op jit(solution)/shard_map/norm/pallas_call | solution.py:257
  (14 shorter events, 0.1 us)
Async XLA Ops:
  0.0 1.1 copy-start.1
  1.1 1.1 copy-start.2
  2.3 0.7 copy-start.3
  7.9 11.8 %copy-start = (bf16[48,64,128]{2,1,0:T(8,128)(2,1)S(1)}, bf16[48,64,128]{2,1,0:T(8,128)(2,1)}, u32[]{:S(2)}) copy-start(bf16[48,64,128]{2,1,0:T(8,128)(2,1)} %queries_ref.1) | copy-start | bytes 2359300
  7.9 11.8 %copy-start.4 = (bf16[48,64]{1,0:T(8,128)(2,1)S(1)}, bf16[48,64]{1,0:T(8,128)(2,1)}, u32[]{:S(2)}) copy-start(bf16[48,64]{1,0:T(8,128)(2,1)} %decay_ref.3) | copy-start | bytes 18436
  7.9 53.8 %all-to-all-start.1 = ((bf16[64,104,128]{2,1,0:T(8,128)(2,1)}), bf16[64,104,128]{2,1,0:T(8,128)(2,1)S(1)}, u32[]{:S(2)}, u32[]{:S(2)}) async-start(bf16[64,104,128]{2,1,0:T(8,128)(2,1)} %pack_kv.1), calls=%async_computation.1 | async-start | bytes 3407872 | tf_op jit(solution)/shard_map/all_to_all | solution.py:292
  61.7 31.4 %all-to-all-start = ((bf16[64,48,128]{2,1,0:T(8,128)(2,1)}), bf16[64,48,128]{2,1,0:T(8,128)(2,1)S(1)}, u32[]{:S(2)}, u32[]{:S(2)}) async-start(bf16[64,48,128]{2,1,0:T(8,128)(2,1)} %pack_q.1), calls=%async_computation | async-start | bytes 1572864 | tf_op jit(solution)/shard_map/all_to_all | solution.py:293
  69.4 6.2 %collective-permute-start = (f32[136,128]{1,0:T(8,128)S(1)}, f32[136,128]{1,0:T(8,128)S(1)}, u32[]{:S(2)}, u32[]{:S(2)}) collective-permute-start(f32[136,128]{1,0:T(8,128)S(1)} %get-tuple-element.14), channel_id=1, source_target_pairs={{0,64},{64,0},{128,192},{192,128},{256,320},{320,256},{384,448},{4... | collective-permute-start | bytes 208904 | tf_op jit(solution)/shard_map/ppermute | solution.py:279
  75.6 7.8 %collective-permute-start.1 = (f32[136,128]{1,0:T(8,128)S(1)}, f32[136,128]{1,0:T(8,128)S(1)}, u32[]{:S(2)}, u32[]{:S(2)}) collective-permute-start(f32[136,128]{1,0:T(8,128)S(1)} %fusion.1), channel_id=1, source_target_pairs={{0,128},{64,192},{128,0},{192,64},{256,384},{320,448},{384,256},{4... | collective-permute-start | bytes 208904 | tf_op jit(solution)/shard_map/ppermute | solution.py:279
  83.4 9.7 %collective-permute-start.2 = (f32[136,128]{1,0:T(8,128)S(1)}, f32[136,128]{1,0:T(8,128)S(1)}, u32[]{:S(2)}, u32[]{:S(2)}) collective-permute-start(f32[136,128]{1,0:T(8,128)S(1)} %fusion), channel_id=1, source_target_pairs={{0,384},{64,448},{128,256},{192,320},{1,385},{65,449},{129,257},{1... | collective-permute-start | bytes 208904 | tf_op jit(solution)/shard_map/ppermute | solution.py:285
  93.1 39.4 %copy-start.5 = (f32[64,128]{1,0:T(8,128)S(1)}, f32[64,128]{1,0:T(8,128)}, u32[]{:S(2)}) copy-start(f32[64,128]{1,0:T(8,128)} %gain_ref.1) | copy-start | bytes 98308
